TPU v7x, 32 devices: a whole 2x2x4 slice. The times are simulated.
32 devices in a mesh: row: 8 (over z, core), col: 4 (over y, x).
Axes of the slice: x: 2, y: 2, z: 4, core: 2. Of those that a mesh axis runs over, the one named last changes fastest.
Arguments:
- amplitudes: bfloat16 [16, 16, 800, 800], P('col', None, 'row'), as said below
- integrals: bfloat16 [16, 16, 800, 800], P('col', None, 'row'), may hold values from -6 to 6
- fock_virtual: bfloat16 [800, 800], replicated, may hold values from -0.21875 to 0.21875
- occ_levels: int32 [16], replicated, may hold values from -12 to -3
- vir_levels: int32 [800], replicated, may hold values from 2 to 21
- ladder_ints: bfloat16 [800, 800, 2, 800], P('row', 'col'), may hold values from -0.0078125 to 0.0078125
Outputs:
- new_amps: bfloat16 [16, 16, 800, 800], P('col', None, 'row')
- ladder: bfloat16 [16, 16, 2, 800], P('col', 'row')
Inputs may be any that keep to these rules, and one draw needn't show every extreme that they name: amplitudes[i, j, a, b] equals amplitudes[j, i, b, a] exactly.
All inputs are finite; a program needn't handle non-finite values.
Results may differ from a plain program's by a relative error of at most 0.0049.
Values may be sent and summed in bfloat16 or wider, within the bound.
A program may use at most 384 MiB of HBM per device.

v0:
```python
import functools

import jax
import jax.numpy as jnp
from jax import lax
from jax.experimental import pallas as pl
from jax.experimental.pallas import tpu as pltpu
from jax.sharding import PartitionSpec as P

level_step = 0.1
MESH = pl.DeviceIdType.MESH
LANES = 128
CHUNK = 8
AHEAD = 4
GROUPS = (2, 5, 6)
F32 = jnp.float32
BF16 = jnp.bfloat16
NT = (((1,), (1,)), ((), ()))


def up(n, m=LANES):
    return -(-n // m) * m


def partner(k, rows, cols, row, col):
    turn = k // cols
    away = rows // 2 + ((turn + 1) // 2) * (1 - 2 * (turn % 2))
    return ((row + away + rows) % rows, (col + k % cols + 1) % cols)


def greet_all(rows, cols, row, col):
    barrier = pltpu.get_barrier_semaphore()
    count = rows * cols

    def greet(k, carry):
        pl.semaphore_signal(
            barrier, inc=1, device_id=partner(k, rows, cols, row, col), device_id_type=MESH
        )
        return carry

    lax.fori_loop(0, count - 1, greet, 0)
    pl.semaphore_wait(barrier, count - 1)


class Sizes:
    pass


def sizes(rows, cols, amplitudes, ladder_ints):
    g = Sizes()
    g.rows, g.cols = rows, cols
    g.o, g.O, g.v, g.V = amplitudes.shape
    g.window = ladder_ints.shape[2]
    g.d = ladder_ints.shape[1]
    g.a = CHUNK
    g.k = -(-g.v // g.a)
    g.wire = up(g.o * g.o * g.v)
    g.pair = g.o * g.O
    g.nk = g.a * g.d
    g.nkp = up(g.nk)
    g.turn_total = g.k * rows * g.a
    starts = [f * g.o * g.v for f in range(g.o)]
    g.order_width = up(g.o * g.v + max(start % LANES for start in starts))
    g.wire = max([g.wire] + [start // LANES * LANES + g.order_width for start in starts])
    g.groups = []
    while sum(g.groups) < g.k:
        want = GROUPS[min(len(g.groups), len(GROUPS) - 1)]
        g.groups.append(min(want, g.k - sum(g.groups)))
    g.left = g.v - (g.k - 1) * g.a
    g.pack = 2 * g.left == g.a
    g.half = up(g.wire // 2)
    g.last = g.half if g.pack else g.wire
    g.each = g.O // rows * g.o
    g.wide = up(g.V, 256)
    g.split_rows = max(t for t in range(16, 401, 16) if g.nk % t == 0)
    return g


def main_kernel(
    g,
    amps_ref, ints_ref, slab_ref, raw_ref, occ_col_ref, vir_row_ref, occ_ref, vir_ref,
    out_ref, wire_ref, ladder_ref,
    got, came, came_col, came_row,
    x_send, x_recv, n_send, n_recv, in_sem, slab_sem, out_sem, turn_sem, wire_sem, end_sem,
):
    rows, cols = g.rows, g.cols
    count = rows * cols
    row, col = lax.axis_index("row"), lax.axis_index("col")
    block_rows = g.a * g.O

    def first(k):
        return jnp.minimum(k * g.a, g.v - g.a)

    def send_blocks(k, width):
        lanes = pl.ds(0, width)

        def begin(t, carry):
            peer_row, peer_col = partner(t, rows, cols, row, col)
            at = pl.multiple_of((k * rows + peer_row) * g.a, g.a)
            pltpu.make_async_remote_copy(
                src_ref=wire_ref.at[peer_col, pl.ds(at, g.a), lanes],
                dst_ref=got.at[k, col * rows + row, :, lanes],
                send_sem=x_send.at[k],
                recv_sem=x_recv.at[k],
                device_id=(peer_row, peer_col),
                device_id_type=MESH,
            ).start()
            return carry

        lax.fori_loop(0, count - 1, begin, 0)
        at = pl.multiple_of((k * rows + row) * g.a, g.a)
        pltpu.make_async_copy(
            wire_ref.at[col, pl.ds(at, g.a), lanes],
            got.at[k, col * rows + row, :, lanes],
            x_recv.at[k],
        ).start()

    def arrived(k, width):
        part = got.at[k, :, :, pl.ds(0, width)]
        pltpu.make_async_copy(part, part, x_recv.at[k]).wait()

    def gone(k, width):
        part = got.at[k, pl.ds(0, count - 1), :, pl.ds(0, width)]
        pltpu.make_async_copy(part, part, x_send.at[k]).wait()

    def turn(order, pick, fock_rows, amp_whole, int_whole, staged):
        def whole(step):
            f, slot = step % g.o, step % 2
            return (
                pltpu.make_async_copy(amps_ref.at[f], amp_whole.at[slot], turn_sem.at[0, slot]),
                pltpu.make_async_copy(ints_ref.at[f], int_whole.at[slot], turn_sem.at[1, slot]),
            )

        steps = len(g.groups) * g.o
        for copy in whole(0):
            copy.start()
        width = cols * g.order_width
        spin = lax.broadcasted_iota(jnp.int32, (g.O, width), 0)
        lane = lax.broadcasted_iota(jnp.int32, (g.O, width), 1)
        offset = lane - (spin // g.o) * g.order_width - (spin % g.o) * g.v

        def order_row(u, carry):
            at = pl.ds(pl.multiple_of(u * g.O, g.O), g.O)
            order[at, :] = jnp.where(offset == u, 1.0, 0.0).astype(BF16)
            return carry

        lax.fori_loop(0, g.v, order_row, 0)
        both = lax.broadcasted_iota(jnp.int32, (2 * g.a, g.V), 0)
        place_of = lax.broadcasted_iota(jnp.int32, (2 * g.a, g.V), 1)
        upper = jnp.where(both >= g.a, 1, 0)
        part = both - upper * g.a
        again = jnp.where(part < g.a - g.left, part + g.left, part) if g.pack else part

        def pick_rows(k, shape):
            def one(n, carry):
                at = pl.ds(pl.multiple_of((k * rows + 2 * n) * g.a, 2 * g.a), 2 * g.a)
                same = place_of - shape - upper * g.v == 2 * n * g.v + first(k)
                pick[at, :] = jnp.where(same, 1.0, 0.0).astype(BF16)
                return carry

            lax.fori_loop(0, rows // 2, one, 0)

        def pick_chunk(k, carry):
            pick_rows(k, part)
            return carry

        lax.fori_loop(0, g.k - 1, pick_chunk, 0)
        pick_rows(g.k - 1, again)
        greet_all(rows, cols, row, col)
        done = 0
        for number, size in enumerate(g.groups):
            height = size * rows * g.a
            at = slice(done * rows * g.a, done * rows * g.a + height)
            staged[:, :height] = jnp.zeros((cols, height, g.wire), BF16)
            fock_rows[:height] = (
                2.0 * jnp.dot(pick[at, :], raw_ref[...], preferred_element_type=F32)
            ).astype(BF16)

            def one(f, carry):
                step = number * g.o + f
                slot = step % 2

                @pl.when(step + 1 < steps)
                def _():
                    for copy in whole(step + 1):
                        copy.start()

                for copy in whole(step):
                    copy.wait()
                turned = lax.dot_general(
                    fock_rows[:height], amp_whole[slot], NT, preferred_element_type=F32
                ) + lax.dot_general(pick[at, :], int_whole[slot], NT, preferred_element_type=F32)
                turned = turned.astype(BF16)
                start = f * (g.o * g.v)
                lanes = pl.ds(pl.multiple_of(start // LANES * LANES, LANES), g.order_width)
                for q in range(cols):
                    piece = jnp.dot(
                        turned,
                        order[:, q * g.order_width : (q + 1) * g.order_width],
                        preferred_element_type=F32,
                    )
                    piece = pltpu.roll(piece, start % LANES, 1)
                    staged[q, :height, lanes] += piece.astype(BF16)
                return carry

            lax.fori_loop(0, g.o, one, 0)
            if g.pack and done + size == g.k:
                over = g.wire - g.half
                tail = slice(height - rows * g.a, height)
                high = lax.broadcasted_iota(jnp.int32, (rows * g.a, over), 0) % g.a < g.a - g.left
                for q in range(cols):
                    staged[q, tail, :over] = jnp.where(
                        high,
                        staged[q, tail, g.half :].astype(F32),
                        staged[q, tail, :over].astype(F32),
                    ).astype(BF16)
            copy = pltpu.make_async_copy(staged.at[:, pl.ds(0, height)], wire_ref.at[:, at], wire_sem)
            copy.start()
            copy.wait()
            for k in range(done, min(done + size, AHEAD)):
                send_blocks(k, g.last if k == g.k - 1 else g.wire)
            done += size

    def rest(
        sent_on, amp_buf, int_buf, slab_buf, split_buf, mirror, mirror_low, total, line, result,
        term_ref, fock_ref, place_ref, base_ref, send_col, send_row,
    ):
        def loads(k, slot):
            at = pl.ds(pl.multiple_of(first(k) * g.O, g.O), block_rows)
            return (
                pltpu.make_async_copy(amps_ref.at[:, at, :], amp_buf.at[slot], in_sem.at[0, slot]),
                pltpu.make_async_copy(ints_ref.at[:, at, :], int_buf.at[slot], in_sem.at[1, slot]),
            )

        def slab_load(k, slot):
            return pltpu.make_async_copy(
                slab_ref.at[pl.ds(first(k) * g.d, g.nk)], slab_buf.at[slot], slab_sem.at[slot]
            )

        def out_store(k, slot):
            at = pl.ds(pl.multiple_of(first(k) * g.O, g.O), block_rows)
            return pltpu.make_async_copy(result.at[slot], out_ref.at[:, at, :], out_sem.at[slot])

        def last_store():
            height = g.left * g.O
            slot = (g.k - 1) % 2
            return pltpu.make_async_copy(
                result.at[slot, :, pl.ds(block_rows - height, height), :],
                out_ref.at[:, pl.ds((g.k - 1) * g.a * g.O, height), :],
                out_sem.at[slot],
            )

        def send_amps(k, slot):
            for n in range(1, cols):
                peer = (col + n) % cols
                pltpu.make_async_remote_copy(
                    src_ref=sent_on.at[slot, peer],
                    dst_ref=came.at[k, col],
                    send_sem=n_send.at[k],
                    recv_sem=n_recv.at[k],
                    device_id=(row, peer),
                    device_id_type=MESH,
                ).start()
            pltpu.make_async_copy(sent_on.at[slot, col], came.at[k, col], n_recv.at[k]).start()

        def all_sent(k, slot):
            part = sent_on.at[slot, pl.ds(0, cols - 1)]
            pltpu.make_async_copy(part, part, n_send.at[k]).wait()

        def combine(k, slot):
            def spread(t, carry):
                at = (t // rows) * g.o
                block = got[k, t].astype(F32)
                for f in range(g.o):
                    for s in range(g.o):
                        start = (f * g.o + s) * g.v
                        tile, phase = start // LANES, start % LANES
                        span = min(tile * LANES + up(phase + g.v), g.wire) - tile * LANES
                        piece = block[:, tile * LANES : tile * LANES + span]
                        if phase:
                            piece = pltpu.roll(piece, span - phase, 1)
                        goal = pl.ds(s * block_rows + at + f, g.a, stride=g.O)
                        mirror[t % rows, goal, :] = piece[:, :LANES]
                return carry

            lax.fori_loop(0, count, spread, 0)
            for n in range(rows):
                mirror_low[:, n * LANES : (n + 1) * LANES] = mirror[n].astype(BF16)
            mine = amp_buf[slot].reshape(g.o * block_rows, g.V)

            def column(n, carry):
                lane = pl.ds(pl.multiple_of(n * 256, 256), 256)
                total[:, lane] = jnp.dot(
                    mirror_low[...], place_ref[:, lane], preferred_element_type=F32
                ) + jnp.dot(mine, fock_ref[:, lane], preferred_element_type=F32)
                return carry

            lax.fori_loop(0, g.wide // 256, column, 0)
            start = first(k)
            lane_of = lax.broadcasted_iota(jnp.int32, (g.pair, LANES), 1)
            for a in range(g.a):
                level = vir_ref[row * g.v + start + a]
                fresh = start + a >= k * g.a
                for i in range(g.o):
                    at = i * block_rows + a * g.O
                    summed = total[at : at + g.O, : g.V] + int_buf[
                        slot, i, a * g.O : (a + 1) * g.O, :
                    ].astype(F32)
                    levels = base_ref[...] + (level - occ_ref[col * g.o + i])
                    value = summed / (levels.astype(F32) * level_step)
                    result[slot, i, a * g.O : (a + 1) * g.O, :] = value.astype(BF16)
                    line[i * g.O : (i + 1) * g.O, : g.V] = jnp.where(fresh, value, 0.0)
                goal = a * g.d
                goal_tile, goal_phase = goal // LANES, goal % LANES
                goal_tiles = up(goal_phase + g.d) // LANES
                for q in range(cols):
                    begin, end = q * g.d, (q + 1) * g.d
                    tiles = max(goal_tiles, -(-end // LANES) - begin // LANES)
                    left = min(begin // LANES, g.wide // LANES - tiles)
                    piece = line[:, left * LANES : (left + tiles) * LANES]
                    shift = (goal_phase - (begin - left * LANES)) % (tiles * LANES)
                    if shift:
                        piece = pltpu.roll(piece, shift, 1)
                    for t in range(goal_tiles):
                        lane = slice((goal_tile + t) * LANES, (goal_tile + t + 1) * LANES)
                        new = piece[:, t * LANES : (t + 1) * LANES]
                        if t == 0 and goal_phase:
                            old = sent_on[slot, q, :, lane].astype(F32)
                            new = jnp.where(lane_of >= goal_phase, new, old)
                        if a == g.a - 1 and t == goal_tiles - 1 and g.nkp > g.nk:
                            new = jnp.where(lane_of < g.nk - (goal_tile + t) * LANES, new, 0.0)
                        sent_on[slot, q, :, lane] = new.astype(BF16)

        def multiply(k, slot):
            pltpu.make_async_copy(came.at[k], came.at[k], n_recv.at[k]).wait()
            slab_load(k, slot).wait()

            def split(m, carry):
                at = pl.ds(pl.multiple_of(m * g.split_rows, 16), g.split_rows)
                parted = pltpu.einshape("tab->atb", slab_buf[slot, at])
                for w in range(g.window):
                    split_buf[w, at, :] = parted[w]
                return carry

            lax.fori_loop(0, g.nk // g.split_rows, split, 0)

            left = came[k].reshape(cols * g.pair, g.nkp)[:, : g.nk]

            def column(w, carry):
                term_ref[w] += jnp.dot(left, split_buf[w], preferred_element_type=F32)
                return carry

            lax.fori_loop(0, g.window, column, 0)

        def reduce():
            for n in range(1, cols):
                peer = (col + n) % cols
                at = pl.ds(pl.multiple_of(peer * g.pair, g.pair), g.pair)
                for w in range(g.window):
                    send_col[n - 1, w] = term_ref[w, at, :].astype(BF16)
                pltpu.make_async_remote_copy(
                    src_ref=send_col.at[n - 1],
                    dst_ref=came_col.at[cols - 1 - n],
                    send_sem=end_sem.at[0],
                    recv_sem=end_sem.at[1],
                    device_id=(row, peer),
                    device_id_type=MESH,
                ).start()
            here = lax.broadcasted_iota(jnp.int32, (g.pair, g.pair), 0)
            there = lax.broadcasted_iota(jnp.int32, (g.pair, g.pair), 1)
            swap = jnp.where(there == (here % g.o) * g.O + here // g.o, 1.0, 0.0).astype(BF16)
            pltpu.make_async_copy(came_col, came_col, end_sem.at[1]).wait()
            at = pl.ds(pl.multiple_of(col * g.pair, g.pair), g.pair)
            for w in range(g.window):
                whole = term_ref[w, at, :]
                for n in range(cols - 1):
                    whole = whole + came_col[n, w].astype(F32)
                whole = jnp.dot(swap, whole.astype(BF16), preferred_element_type=F32)
                for n in range(rows):
                    send_row[n, w] = whole[n * g.each : (n + 1) * g.each].astype(BF16)
            for n in range(1, rows):
                peer = (row + n) % rows
                pltpu.make_async_remote_copy(
                    src_ref=send_row.at[peer],
                    dst_ref=came_row.at[rows - 1 - n],
                    send_sem=end_sem.at[2],
                    recv_sem=end_sem.at[3],
                    device_id=(peer, col),
                    device_id_type=MESH,
                ).start()
            pltpu.make_async_copy(came_row, came_row, end_sem.at[3]).wait()
            for w in range(g.window):
                whole = send_row[row, w].astype(F32)
                for n in range(rows - 1):
                    whole = whole + came_row[n, w].astype(F32)
                ladder_ref[w] = whole
            pltpu.make_async_copy(send_col, send_col, end_sem.at[0]).wait()
            part = send_row.at[pl.ds(0, rows - 1)]
            pltpu.make_async_copy(part, part, end_sem.at[2]).wait()

        for copy in loads(0, 0):
            copy.start()
        for k in range(min(2, g.k)):
            slab_load(k, k).start()
        fock_ref[...] = jnp.zeros_like(fock_ref)
        fock_ref[:, : g.V] = (2.0 * jnp.transpose(raw_ref[...].astype(F32))).astype(BF16)
        down = lax.broadcasted_iota(jnp.int32, (LANES, g.wide), 0)
        gap = lax.broadcasted_iota(jnp.int32, (LANES, g.wide), 1) - down
        for n in range(rows):
            same = jnp.logical_and(gap == n * g.v, down < g.v)
            place_ref[n * LANES : (n + 1) * LANES, :] = jnp.where(same, 1.0, 0.0).astype(BF16)
        base_ref[...] = vir_row_ref[...] - occ_col_ref[...]
        term_ref[...] = jnp.zeros_like(term_ref)
        line[...] = jnp.zeros_like(line)

        def chunk(k, carry):
            slot = k % 2

            @pl.when(k + AHEAD == g.k - 1)
            def _():
                send_blocks(g.k - 1, g.last)

            @pl.when(k + AHEAD < g.k - 1)
            def _():
                send_blocks(k + AHEAD, g.wire)

            @pl.when(k + 1 < g.k)
            def _():
                for copy in loads(k + 1, (k + 1) % 2):
                    copy.start()

            for copy in loads(k, slot):
                copy.wait()

            @pl.when(k < g.k - 1)
            def _():
                arrived(k, g.wire)

            @pl.when(k == g.k - 1)
            def _():
                arrived(g.k - 1, g.last)
                if g.pack:
                    over = g.wire - g.half

                    def unpack(t, carry):
                        block = got[g.k - 1, t, :, : g.half].astype(F32)
                        block = pltpu.roll(block, g.a - g.left, 0)
                        got[g.k - 1, t, :, g.half :] = block[:, :over].astype(BF16)
                        return carry

                    lax.fori_loop(0, count, unpack, 0)


            @pl.when(k >= 2)
            def _():
                all_sent(k - 2, slot)

            combine(k, slot)
            send_amps(k, slot)

            @pl.when(k >= 1)
            def _():
                out_store(k - 1, (k + 1) % 2).wait()

            @pl.when(k < g.k - 1)
            def _():
                out_store(k, slot).start()

            @pl.when(k == g.k - 1)
            def _():
                last_store().start()

            @pl.when(k >= 1)
            def _():
                multiply(k - 1, (k + 1) % 2)

                @pl.when(k + 1 < g.k)
                def _():
                    slab_load(k + 1, (k + 1) % 2).start()

            return carry

        lax.fori_loop(0, g.k, chunk, 0)
        multiply(g.k - 1, (g.k - 1) % 2)
        for k in range(max(0, g.k - 2), g.k):
            all_sent(k, k % 2)
        reduce()
        last_store().wait()

        def drain(k, carry):
            gone(k, g.wire)
            return carry

        lax.fori_loop(0, g.k - 1, drain, 0)
        gone(g.k - 1, g.last)
    slots = 2
    pl.run_scoped(
        turn,
        pltpu.VMEM((g.v * g.O, cols * g.order_width), BF16),
        pltpu.VMEM((g.turn_total, g.V), BF16),
        pltpu.VMEM((max(g.groups) * rows * g.a, g.V), BF16),
        pltpu.VMEM((slots, g.v * g.O, g.V), BF16),
        pltpu.VMEM((slots, g.v * g.O, g.V), BF16),
        pltpu.VMEM((cols, max(g.groups) * rows * g.a, g.wire), BF16),
    )
    pl.run_scoped(
        rest,
        pltpu.VMEM((2, g.cols, g.pair, g.nkp), BF16),
        pltpu.VMEM((2, g.o, block_rows, g.V), BF16),
        pltpu.VMEM((2, g.o, block_rows, g.V), BF16),
        pltpu.VMEM((2, g.nk, g.window, g.V), BF16),
        pltpu.VMEM((g.window, g.nk, g.V), BF16),
        pltpu.VMEM((g.rows, g.o * block_rows, LANES), F32),
        pltpu.VMEM((g.o * block_rows, g.rows * LANES), BF16),
        pltpu.VMEM((g.o * block_rows, g.wide), F32),
        pltpu.VMEM((g.pair, g.wide), F32),
        pltpu.VMEM((2, g.o, block_rows, g.V), BF16),
        pltpu.VMEM((g.window, cols * g.pair, g.V), F32),
        pltpu.VMEM((g.V, g.wide), BF16),
        pltpu.VMEM((rows * LANES, g.wide), BF16),
        pltpu.VMEM((g.O, g.V), jnp.int32),
        pltpu.VMEM((cols - 1, g.window, g.pair, g.V), BF16),
        pltpu.VMEM((rows, g.window, g.each, g.V), BF16),
    )


def main_call(g, amps, ints, slab, fock_virtual, occ_levels, vir_levels):
    count = g.rows * g.cols
    any_space = pl.BlockSpec(memory_space=pl.ANY)
    vmem = pl.BlockSpec(memory_space=pltpu.VMEM)
    smem = pl.BlockSpec(memory_space=pltpu.SMEM)
    dma = pltpu.SemaphoreType.DMA
    out, _, ladder = pl.pallas_call(
        functools.partial(main_kernel, g),
        out_shape=(
            jax.ShapeDtypeStruct((g.o, g.v * g.O, g.V), BF16),
            jax.ShapeDtypeStruct((g.cols, g.turn_total, g.wire), BF16),
            jax.ShapeDtypeStruct((g.window, g.each, g.V), F32),
        ),
        in_specs=[any_space] * 3 + [vmem] * 3 + [smem] * 2,
        out_specs=(any_space, any_space, vmem),
        scratch_shapes=[
            pltpu.VMEM((g.k, count, g.a, g.wire), BF16),
            pltpu.VMEM((g.k, g.cols, g.pair, g.nkp), BF16),
            pltpu.VMEM((g.cols - 1, g.window, g.pair, g.V), BF16),
            pltpu.VMEM((g.rows - 1, g.window, g.each, g.V), BF16),
            dma((g.k,)), dma((g.k,)), dma((g.k,)), dma((g.k,)),
            dma((2, 2)), dma((2,)), dma((2,)), dma((2, 2)), dma(()), dma((4,)),
        ],
        compiler_params=pltpu.CompilerParams(
            collective_id=0, has_side_effects=True, vmem_limit_bytes=67_000_000
        ),
    )(
        amps, ints, slab, fock_virtual, occ_levels.reshape(g.O, 1), vir_levels.reshape(1, g.V),
        occ_levels, vir_levels,
    )
    return out, ladder


def body(rows, cols, amplitudes, integrals, fock_virtual, occ_levels, vir_levels, ladder_ints):
    g = sizes(rows, cols, amplitudes, ladder_ints)
    amps = jnp.transpose(amplitudes, (0, 2, 1, 3)).reshape(g.o, g.v * g.O, g.V)
    ints = jnp.transpose(integrals, (0, 2, 1, 3)).reshape(g.o, g.v * g.O, g.V)
    slab = ladder_ints.reshape(g.v * g.d, g.window, g.V)
    result, ladder = main_call(g, amps, ints, slab, fock_virtual, occ_levels, vir_levels)
    new_amps = jnp.transpose(result.reshape(g.o, g.v, g.O, g.V), (0, 2, 1, 3))
    ladder = ladder.reshape(g.window, g.O // rows, g.o, g.V)
    return (new_amps, jnp.transpose(ladder, (2, 1, 0, 3)).astype(BF16))


def solution(mesh):
    placed = (
        P("col", None, "row", None),
        P("col", None, "row", None),
        P(),
        P(),
        P(),
        P("row", "col", None, None),
    )
    return jax.shard_map(
        functools.partial(body, mesh.shape["row"], mesh.shape["col"]),
        mesh=mesh,
        in_specs=placed,
        out_specs=(P("col", None, "row", None), P("col", "row", None, None)),
        check_vma=False,
    )
```

profile of v0, /device:TPU:0, one launch (start us, length us, event | category | flops | bytes accessed | tf_op | source)
XLA Modules:
  0.0 329.0 jit_solution(13677271154517895149)
XLA Ops:
  0.6 1.3 reshape.28.vir_row_ref
  1.9 1.3 copy.8.occ_col_ref
  3.2 313.9 %shard_map.77 = (bf16[4,1600,800]{2,1,0:T(8,128)(2,1)}, bf16[4,832,1664]{2,1,0:T(8,128)(2,1)}, f32[2,8,800]{2,1,0:T(8,128)}) custom-call(bf16[4,1600,800]{2,1,0:T(8,128)(2,1)} %bitcast.15, bf16[4,1600,800]{2,1,0:T(8,128)(2,1)} %bitcast.16, bf16[20000,2,800]{2,1,0:T(2,128)(2,1)} %bitcast.4.slab_ref, bf16[800,800]{1,0:T(8,128)(2,1)} %raw_ref.1, ...), custom_call_target="tpu_custom_call" | custom-call | tf_op jit(solution)/shard_map/pallas_call | solution.py:533
  317.1 0.8 convert_element_type.9
  318.0 0.6 copy.11
  318.6 10.4 %copy.13 = bf16[4,16,100,800]{3,1,2,0:T(8,128)(2,1)} copy(bf16[4,16,100,800]{3,1,2,0:T(8,128)(2,1)} %bitcast.14) | data formatting | bytes 20480000
  (1 shorter events, 0.0 us)
where the time goes:
time: 329 us
  Pallas kernels  314 us (95%)
  local copies, waits for them, and re-layouts  13.7 us (4%)
    pallas_call x1, Pallas kernels, main_call(): pl.pallas_call(functools.partial(main_kernel, g), out_shape=(jax.ShapeDty...  314 us
    unnamed x1, local copies, waits for them, and re-layouts  10.4 us

commit v1 on v0

--- a/solution.py
+++ b/solution.py
@@ -12,7 +12,8 @@
 LANES = 128
 CHUNK = 8
 AHEAD = 4
-GROUPS = (2, 5, 6)
+GROUPS = (1, 3, 4, 5)
+PLANE = 2
 F32 = jnp.float32
 BF16 = jnp.bfloat16
 NT = (((1,), (1,)), ((), ()))
@@ -91,23 +92,39 @@
     def first(k):
         return jnp.minimum(k * g.a, g.v - g.a)
 
-    def send_blocks(k, width):
+    planes = rows // PLANE
+
+    def send_block(k, width, peer_row, peer_col):
         lanes = pl.ds(0, width)
-
+        at = pl.multiple_of((k * rows + peer_row) * g.a, g.a)
+        pltpu.make_async_remote_copy(
+            src_ref=wire_ref.at[peer_col, pl.ds(at, g.a), lanes],
+            dst_ref=got.at[k, col * rows + row, :, lanes],
+            send_sem=x_send.at[k],
+            recv_sem=x_recv.at[k],
+            device_id=(peer_row, peer_col),
+            device_id_type=MESH,
+        ).start()
+
+    def send_far(k, width):
         def begin(t, carry):
-            peer_row, peer_col = partner(t, rows, cols, row, col)
-            at = pl.multiple_of((k * rows + peer_row) * g.a, g.a)
-            pltpu.make_async_remote_copy(
-                src_ref=wire_ref.at[peer_col, pl.ds(at, g.a), lanes],
-                dst_ref=got.at[k, col * rows + row, :, lanes],
-                send_sem=x_send.at[k],
-                recv_sem=x_recv.at[k],
-                device_id=(peer_row, peer_col),
-                device_id_type=MESH,
-            ).start()
+            turn = t // (PLANE * cols)
+            away = planes // 2 + ((turn + 1) // 2) * (1 - 2 * (turn % 2))
+            plane = (row // PLANE + away + planes) % planes
+            core = (t // cols) % PLANE
+            send_block(k, width, plane * PLANE + core, (col + t % cols + 1) % cols)
             return carry
 
-        lax.fori_loop(0, count - 1, begin, 0)
+        lax.fori_loop(0, (planes - 1) * PLANE * cols, begin, 0)
+
+    def send_near(k, width):
+        def begin(t, carry):
+            core = (row % PLANE + t // cols + 1) % PLANE
+            send_block(k, width, row // PLANE * PLANE + core, (col + t % cols + 1) % cols)
+            return carry
+
+        lax.fori_loop(0, PLANE * cols - 1, begin, 0)
+        lanes = pl.ds(0, width)
         at = pl.multiple_of((k * rows + row) * g.a, g.a)
         pltpu.make_async_copy(
             wire_ref.at[col, pl.ds(at, g.a), lanes],
@@ -217,8 +234,11 @@
             copy = pltpu.make_async_copy(staged.at[:, pl.ds(0, height)], wire_ref.at[:, at], wire_sem)
             copy.start()
             copy.wait()
-            for k in range(done, min(done + size, AHEAD)):
-                send_blocks(k, g.last if k == g.k - 1 else g.wire)
+            for k in range(done, done + size):
+                width = g.last if k == g.k - 1 else g.wire
+                if k < AHEAD:
+                    send_far(k, width)
+                send_near(k, width)
             done += size
 
     def rest(
@@ -250,21 +270,23 @@
                 out_sem.at[slot],
             )
 
-        def send_amps(k, slot):
+        def send_amps(k, slot, lanes):
             for n in range(1, cols):
                 peer = (col + n) % cols
                 pltpu.make_async_remote_copy(
-                    src_ref=sent_on.at[slot, peer],
-                    dst_ref=came.at[k, col],
+                    src_ref=sent_on.at[slot, peer, :, lanes],
+                    dst_ref=came.at[k, col, :, lanes],
                     send_sem=n_send.at[k],
                     recv_sem=n_recv.at[k],
                     device_id=(row, peer),
                     device_id_type=MESH,
                 ).start()
-            pltpu.make_async_copy(sent_on.at[slot, col], came.at[k, col], n_recv.at[k]).start()
-
-        def all_sent(k, slot):
-            part = sent_on.at[slot, pl.ds(0, cols - 1)]
+            pltpu.make_async_copy(
+                sent_on.at[slot, col, :, lanes], came.at[k, col, :, lanes], n_recv.at[k]
+            ).start()
+
+        def all_sent(k, slot, lanes):
+            part = sent_on.at[slot, pl.ds(0, cols - 1), :, lanes]
             pltpu.make_async_copy(part, part, n_send.at[k]).wait()
 
         def combine(k, slot):
@@ -331,8 +353,15 @@
                             new = jnp.where(lane_of < g.nk - (goal_tile + t) * LANES, new, 0.0)
                         sent_on[slot, q, :, lane] = new.astype(BF16)
 
-        def multiply(k, slot):
-            pltpu.make_async_copy(came.at[k], came.at[k], n_recv.at[k]).wait()
+        stale = (g.a - g.left) * g.d // LANES * LANES
+        every = pl.ds(0, g.nkp)
+        valid = pl.ds(stale, g.nkp - stale)
+        if stale:
+            came[g.k - 1, :, :, :stale] = jnp.zeros((cols, g.pair, stale), BF16)
+
+        def multiply(k, slot, lanes):
+            part = came.at[k, :, :, lanes]
+            pltpu.make_async_copy(part, part, n_recv.at[k]).wait()
             slab_load(k, slot).wait()
 
             def split(m, carry):
@@ -418,11 +447,11 @@
 
             @pl.when(k + AHEAD == g.k - 1)
             def _():
-                send_blocks(g.k - 1, g.last)
+                send_far(g.k - 1, g.last)
 
             @pl.when(k + AHEAD < g.k - 1)
             def _():
-                send_blocks(k + AHEAD, g.wire)
+                send_far(k + AHEAD, g.wire)
 
             @pl.when(k + 1 < g.k)
             def _():
@@ -453,10 +482,16 @@
 
             @pl.when(k >= 2)
             def _():
-                all_sent(k - 2, slot)
+                all_sent(k - 2, slot, every)
 
             combine(k, slot)
-            send_amps(k, slot)
+            @pl.when(k < g.k - 1)
+            def _():
+                send_amps(k, slot, every)
+
+            @pl.when(k == g.k - 1)
+            def _():
+                send_amps(g.k - 1, slot, valid)
 
             @pl.when(k >= 1)
             def _():
@@ -472,7 +507,7 @@
 
             @pl.when(k >= 1)
             def _():
-                multiply(k - 1, (k + 1) % 2)
+                multiply(k - 1, (k + 1) % 2, every)
 
                 @pl.when(k + 1 < g.k)
                 def _():
@@ -481,9 +516,9 @@
             return carry
 
         lax.fori_loop(0, g.k, chunk, 0)
-        multiply(g.k - 1, (g.k - 1) % 2)
+        multiply(g.k - 1, (g.k - 1) % 2, valid)
         for k in range(max(0, g.k - 2), g.k):
-            all_sent(k, k % 2)
+            all_sent(k, k % 2, valid if k == g.k - 1 else every)
         reduce()
         last_store().wait()
 

time: 329 us -> 318 us (0.967)
  Pallas kernels: 314 us -> 302 us
    pallas_call x1, Pallas kernels: 314 us -> 302 us  [main_call(): pl.pallas_call(functools.partial(main_kernel, g), out_shape=(jax.ShapeDty...]
where the time goes in v1:
time: 318 us; the launch traced here: 317 us
  Pallas kernels  302 us (95%)
  local copies, waits for them, and re-layouts  13.7 us (4%)
    pallas_call x1, Pallas kernels, main_call(): pl.pallas_call(functools.partial(main_kernel, g), out_shape=(jax.ShapeDty...  302 us
    unnamed x1, local copies, waits for them, and re-layouts  10.4 us

profile of v1, /device:TPU:0, one launch (start us, length us, event | category | flops | bytes accessed | tf_op | source)
XLA Modules:
  0.0 317.3 jit_solution(11257546614273790668)
XLA Ops:
  0.6 1.3 reshape.28.vir_row_ref
  1.9 1.3 copy.8.occ_col_ref
  3.2 302.1 %shard_map.77 = (bf16[4,1600,800]{2,1,0:T(8,128)(2,1)}, bf16[4,832,1664]{2,1,0:T(8,128)(2,1)}, f32[2,8,800]{2,1,0:T(8,128)}) custom-call(bf16[4,1600,800]{2,1,0:T(8,128)(2,1)} %bitcast.15, bf16[4,1600,800]{2,1,0:T(8,128)(2,1)} %bitcast.16, bf16[20000,2,800]{2,1,0:T(2,128)(2,1)} %bitcast.4.slab_ref, bf16[800,800]{1,0:T(8,128)(2,1)} %raw_ref.1, ...), custom_call_target="tpu_custom_call" | custom-call | tf_op jit(solution)/shard_map/pallas_call | solution.py:568
  305.4 0.8 convert_element_type.9
  306.2 0.6 copy.11
  306.8 10.4 %copy.13 = bf16[4,16,100,800]{3,1,2,0:T(8,128)(2,1)} copy(bf16[4,16,100,800]{3,1,2,0:T(8,128)(2,1)} %bitcast.14) | data formatting | bytes 20480000
  (1 shorter events, 0.0 us)

commit v2 on v1

--- a/solution.py
+++ b/solution.py
@@ -12,6 +12,7 @@
 LANES = 128
 CHUNK = 8
 AHEAD = 4
+HOLD = 3
 GROUPS = (1, 3, 4, 5)
 PLANE = 2
 F32 = jnp.float32
@@ -290,6 +291,7 @@
             pltpu.make_async_copy(part, part, n_send.at[k]).wait()
 
         def combine(k, slot):
+            hold = k % HOLD
             def spread(t, carry):
                 at = (t // rows) * g.o
                 block = got[k, t].astype(F32)
@@ -347,11 +349,11 @@
                         lane = slice((goal_tile + t) * LANES, (goal_tile + t + 1) * LANES)
                         new = piece[:, t * LANES : (t + 1) * LANES]
                         if t == 0 and goal_phase:
-                            old = sent_on[slot, q, :, lane].astype(F32)
+                            old = sent_on[hold, q, :, lane].astype(F32)
                             new = jnp.where(lane_of >= goal_phase, new, old)
                         if a == g.a - 1 and t == goal_tiles - 1 and g.nkp > g.nk:
                             new = jnp.where(lane_of < g.nk - (goal_tile + t) * LANES, new, 0.0)
-                        sent_on[slot, q, :, lane] = new.astype(BF16)
+                        sent_on[hold, q, :, lane] = new.astype(BF16)
 
         stale = (g.a - g.left) * g.d // LANES * LANES
         every = pl.ds(0, g.nkp)
@@ -480,18 +482,18 @@
                     lax.fori_loop(0, count, unpack, 0)
 
 
-            @pl.when(k >= 2)
-            def _():
-                all_sent(k - 2, slot, every)
+            @pl.when(k >= HOLD)
+            def _():
+                all_sent(k - HOLD, k % HOLD, every)
 
             combine(k, slot)
             @pl.when(k < g.k - 1)
             def _():
-                send_amps(k, slot, every)
+                send_amps(k, k % HOLD, every)
 
             @pl.when(k == g.k - 1)
             def _():
-                send_amps(g.k - 1, slot, valid)
+                send_amps(g.k - 1, (g.k - 1) % HOLD, valid)
 
             @pl.when(k >= 1)
             def _():
@@ -505,20 +507,18 @@
             def _():
                 last_store().start()
 
-            @pl.when(k >= 1)
-            def _():
-                multiply(k - 1, (k + 1) % 2, every)
-
-                @pl.when(k + 1 < g.k)
-                def _():
-                    slab_load(k + 1, (k + 1) % 2).start()
+            @pl.when(k >= 2)
+            def _():
+                multiply(k - 2, slot, every)
+                slab_load(k, slot).start()
 
             return carry
 
         lax.fori_loop(0, g.k, chunk, 0)
-        multiply(g.k - 1, (g.k - 1) % 2, valid)
         for k in range(max(0, g.k - 2), g.k):
-            all_sent(k, k % 2, valid if k == g.k - 1 else every)
+            multiply(k, k % 2, valid if k == g.k - 1 else every)
+        for k in range(max(0, g.k - HOLD), g.k):
+            all_sent(k, k % HOLD, valid if k == g.k - 1 else every)
         reduce()
         last_store().wait()
 
@@ -540,7 +540,7 @@
     )
     pl.run_scoped(
         rest,
-        pltpu.VMEM((2, g.cols, g.pair, g.nkp), BF16),
+        pltpu.VMEM((HOLD, g.cols, g.pair, g.nkp), BF16),
         pltpu.VMEM((2, g.o, block_rows, g.V), BF16),
         pltpu.VMEM((2, g.o, block_rows, g.V), BF16),
         pltpu.VMEM((2, g.nk, g.window, g.V), BF16),

time: 318 us -> 314 us (0.987)
  no operation moved by 1% of the time
where the time goes in v2:
time: 314 us
  Pallas kernels  299 us (95%)
  local copies, waits for them, and re-layouts  13.7 us (4%)
    pallas_call x1, Pallas kernels, main_call(): pl.pallas_call(functools.partial(main_kernel, g), out_shape=(jax.ShapeDty...  299 us
    unnamed x1, local copies, waits for them, and re-layouts  10.4 us

profile of v2, /device:TPU:0, one launch (start us, length us, event | category | flops | bytes accessed | tf_op | source)
XLA Modules:
  0.0 314.1 jit_solution(7083612658886002307)
XLA Ops:
  0.6 1.3 reshape.28.vir_row_ref
  1.9 1.3 copy.8.occ_col_ref
  3.2 299.0 %shard_map.77 = (bf16[4,1600,800]{2,1,0:T(8,128)(2,1)}, bf16[4,832,1664]{2,1,0:T(8,128)(2,1)}, f32[2,8,800]{2,1,0:T(8,128)}) custom-call(bf16[4,1600,800]{2,1,0:T(8,128)(2,1)} %bitcast.15, bf16[4,1600,800]{2,1,0:T(8,128)(2,1)} %bitcast.16, bf16[20000,2,800]{2,1,0:T(2,128)(2,1)} %bitcast.4.slab_ref, bf16[800,800]{1,0:T(8,128)(2,1)} %raw_ref.1, ...), custom_call_target="tpu_custom_call" | custom-call | tf_op jit(solution)/shard_map/pallas_call | solution.py:568
  302.2 0.8 convert_element_type.9
  303.1 0.6 copy.11
  303.7 10.4 %copy.13 = bf16[4,16,100,800]{3,1,2,0:T(8,128)(2,1)} copy(bf16[4,16,100,800]{3,1,2,0:T(8,128)(2,1)} %bitcast.14) | data formatting | bytes 20480000
  (1 shorter events, 0.0 us)
